TPU v7x, 512 devices: a whole 4x4x16 slice. The times are simulated.
512 devices in a mesh: dp: 32 (over y_lo, z), tensor: 16 (over y_hi, x, core).
Axes of the slice: x: 4, y: 4 (y_hi: 2, y_lo: 2; y = y_hi * 2 + y_lo), z: 16, core: 2. Of those that a mesh axis runs over, the one named last changes fastest.
Arguments:
- inputs: bfloat16 [4096, 8192], P('dp', 'tensor'), may hold values from -6 to 6
- grad_context: bfloat16 [4096, 8192], P('dp', 'tensor'), may hold values from -24 to 24
- gain: float32 [8192], replicated, may hold values from 0.1 to 1.9
- w_query: bfloat16 [8192, 8192], P('dp', 'tensor'), may hold values from -0.0625 to 0.0625
- w_keyval: bfloat16 [8192, 1024], P('dp', 'tensor'), may hold values from -0.0625 to 0.0625
Outputs:
- grad_input: bfloat16 [4096, 8192], P('dp', 'tensor')
- grad_gain: float32 [8192], P('tensor')
- grad_w_keyval: bfloat16 [8192, 1024], P('dp', 'tensor')
All inputs are finite; a program needn't handle non-finite values.
Results may differ from a plain program's by a relative error of at most 0.023.
Values may be sent and summed in bfloat16 or wider, within the bound.
A program may use at most 64 MiB of HBM per device.

v0:
```python
import math
import jax
import jax.numpy as jnp
from jax import lax
from jax.sharding import PartitionSpec as P

HD = 128
KV_HEADS = 4
HEADS_DEV = 4


def rope_tables(length, head_size):
    positions = lax.broadcasted_iota(jnp.int32, (length, head_size // 2), 0).astype(jnp.float32)
    index_half = lax.broadcasted_iota(jnp.int32, (length, head_size // 2), 1).astype(jnp.float32)
    frequency = jnp.exp(-(2.0 * index_half / head_size) * math.log(500000.0))
    angles = positions * frequency
    return (jnp.cos(angles), jnp.sin(angles))


def rotate(vectors, cosine_table, sine_table):
    half_size = vectors.shape[-1] // 2
    first_half = vectors[..., :half_size]
    second_half = vectors[..., half_size:]
    return jnp.concatenate(
        [
            first_half * cosine_table - second_half * sine_table,
            first_half * sine_table + second_half * cosine_table,
        ],
        axis=-1,
    )


def unrotate(vectors, cosine_table, sine_table):
    half_size = vectors.shape[-1] // 2
    first_half = vectors[..., :half_size]
    second_half = vectors[..., half_size:]
    return jnp.concatenate(
        [
            first_half * cosine_table + second_half * sine_table,
            second_half * cosine_table - first_half * sine_table,
        ],
        axis=-1,
    )


def on_device(inputs, grad_context, gain, w_query, w_keyval):
    contract_last = (((1,), (1,)), ((), ()))
    contract_first = (((0,), (0,)), ((), ()))
    seq_length = inputs.shape[0]
    local_cols = inputs.shape[1]
    model_width = gain.shape[0]
    head_size = HD
    heads_here = HEADS_DEV
    group_cols = w_keyval.shape[1]
    tensor_count = lax.axis_size("tensor")
    keyval_total = group_cols * tensor_count
    kv_heads = KV_HEADS
    devices_per_group = tensor_count // kv_heads
    score_scale = head_size ** (-0.5)
    tensor_slot = lax.axis_index("tensor")
    gain_local = lax.dynamic_slice_in_dim(gain, tensor_slot * local_cols, local_cols, 0)
    as_float = inputs.astype(jnp.float32)
    row_sum = lax.psum(jnp.sum(as_float * as_float, axis=1, keepdims=True), "tensor")
    inv_rms = lax.rsqrt(row_sum / model_width + 1e-05)
    unit_rows = as_float * inv_rms
    normed = (unit_rows * gain_local).astype(jnp.bfloat16)
    normed_full = lax.all_gather(normed, "tensor", axis=1, tiled=True)
    query_weight, keyweight = (
        lax.all_gather(w_query, "dp", axis=0, tiled=True),
        lax.all_gather(w_keyval, "dp", axis=0, tiled=True),
    )
    query_proj = jnp.dot(normed_full, query_weight, preferred_element_type=jnp.float32).astype(
        jnp.bfloat16
    )
    keyval_part = jnp.dot(normed_full, keyweight, preferred_element_type=jnp.float32).astype(
        jnp.bfloat16
    )
    keyval_full = lax.all_gather(keyval_part, "tensor", axis=1, tiled=True)
    group_slot = tensor_slot // devices_per_group
    key_block = lax.dynamic_slice_in_dim(keyval_full, group_slot * head_size, head_size, 1)
    value_block = lax.dynamic_slice_in_dim(
        keyval_full, (kv_heads + group_slot) * head_size, head_size, 1
    )
    cosine_table, sine_table = rope_tables(seq_length, head_size)
    cos_heads = cosine_table[:, None, :]
    sin_heads = sine_table[:, None, :]
    query_heads = query_proj.astype(jnp.float32).reshape(seq_length, heads_here, head_size)
    q_rot = rotate(query_heads, cos_heads, sin_heads).astype(jnp.bfloat16)
    k_rot = rotate(key_block.astype(jnp.float32), cosine_table, sine_table).astype(jnp.bfloat16)
    scores = (
        jnp.einsum("shd,td->hst", q_rot, k_rot, preferred_element_type=jnp.float32) * score_scale
    )
    causal = lax.broadcasted_iota(jnp.int32, (seq_length, seq_length), 0) >= lax.broadcasted_iota(
        jnp.int32, (seq_length, seq_length), 1
    )
    exponent = jnp.where(causal[None, :, :], jnp.exp(scores), 0.0)
    softmax_probs = exponent / jnp.sum(exponent, axis=2, keepdims=True)
    prob_weights = softmax_probs.astype(jnp.bfloat16)
    context = jnp.einsum(
        "hst,td->shd", prob_weights, value_block, preferred_element_type=jnp.float32
    ).astype(jnp.bfloat16)
    grad_ctx = grad_context.reshape(seq_length, heads_here, head_size)
    grad_probs = jnp.einsum(
        "shd,td->hst", grad_ctx, value_block, preferred_element_type=jnp.float32
    )
    row_delta = jnp.sum(grad_ctx.astype(jnp.float32) * context.astype(jnp.float32), axis=2).T[
        :, :, None
    ]
    grad_scores = (softmax_probs * (grad_probs - row_delta) * score_scale).astype(jnp.bfloat16)
    grad_qrot = jnp.einsum("hst,td->shd", grad_scores, k_rot, preferred_element_type=jnp.float32)
    grad_krot = jnp.einsum("hst,shd->td", grad_scores, q_rot, preferred_element_type=jnp.float32)
    grad_value = jnp.einsum(
        "hst,shd->td", prob_weights, grad_ctx, preferred_element_type=jnp.float32
    )
    grad_query = (
        unrotate(grad_qrot, cos_heads, sin_heads)
        .astype(jnp.bfloat16)
        .reshape(seq_length, heads_here * head_size)
    )
    grad_terms = jnp.zeros((seq_length, keyval_total), jnp.float32)
    grad_terms = lax.dynamic_update_slice_in_dim(
        grad_terms, unrotate(grad_krot, cosine_table, sine_table), group_slot * head_size, 1
    )
    grad_terms = lax.dynamic_update_slice_in_dim(
        grad_terms, grad_value, (kv_heads + group_slot) * head_size, 1
    )
    grad_keyval = lax.psum_scatter(
        grad_terms.astype(jnp.bfloat16), "tensor", scatter_dimension=1, tiled=True
    )
    result = lax.dot_general(
        query_weight, grad_query, contract_last, preferred_element_type=jnp.float32
    )
    grad_normed = (
        lax.psum_scatter(
            (
                result
                + lax.dot_general(
                    keyweight, grad_keyval, contract_last, preferred_element_type=jnp.float32
                )
            ).astype(jnp.bfloat16),
            "tensor",
            scatter_dimension=0,
            tiled=True,
        )
        .astype(jnp.float32)
        .T
    )
    scaled_grad = grad_normed * gain_local
    product_sum = lax.psum(jnp.sum(scaled_grad * unit_rows, axis=1, keepdims=True), "tensor")
    grad_input = (inv_rms * (scaled_grad - unit_rows * (product_sum / model_width))).astype(
        jnp.bfloat16
    )
    grad_gain = lax.psum(jnp.sum(grad_normed * unit_rows, axis=0), "dp")
    keyval_all = lax.all_gather(grad_keyval, "dp", axis=0, tiled=True)
    rows_normed = lax.all_to_all(normed_full, "dp", split_axis=1, concat_axis=0, tiled=True)
    keyval_weight_grad = lax.dot_general(
        rows_normed, keyval_all, contract_first, preferred_element_type=jnp.float32
    )
    return (grad_input, grad_gain, keyval_weight_grad.astype(jnp.bfloat16))


def solution(mesh):
    in_specs = (P("dp", "tensor"), P("dp", "tensor"), P(), P("dp", "tensor"), P("dp", "tensor"))
    out_specs = (P("dp", "tensor"), P("tensor"), P("dp", "tensor"))
    return jax.shard_map(
        on_device, mesh=mesh, in_specs=in_specs, out_specs=out_specs, check_vma=False
    )
```

profile of v0, /device:TPU:16, one launch (start us, length us, event | category | flops | bytes accessed | tf_op | source)
XLA Modules:
  0.0 727.8 jit_solution(10159442751413504950)
XLA Ops:
  7.2 0.0 all-gather.4.cloned.1.call-start
  7.2 1.0 fusion.25
  8.2 35.1 %psum.21 = f32[128,1]{0,1:T(1,128)S(1)} all-reduce(f32[128,1]{0,1:T(1,128)S(1)} %bitcast.94), channel_id=1, replica_groups=mesh['dp'=32,'tensor'=16] {'tensor'}, use_global_device_ids=true, to_apply=%region_1.0 | all-reduce | flops 128 | bytes 1024 | tf_op jit(solution)/shard_map/psum | solution.py:63
  43.4 0.8 dynamic_slice.9
  44.1 1.7 fusion.19
  45.8 0.0 all-gather.6.cloned.1.call-start
  45.9 0.7 all-gather.6.cloned.1.call-update
  46.6 0.0 all-gather.8.cloned.1.call-start
  46.6 0.7 all-gather.8.cloned.1.call-update
  47.3 63.7 %all-gather.4.cloned.1.call-done = bf16[128,8192]{1,0:T(8,128)(2,1)} async-done(((bf16[128,512]{1,0:T(8,128)(2,1)}), bf16[128,8192]{1,0:T(8,128)(2,1)}) %all-gather.4.cloned.1.call-update) | async-done | bytes 2097168 | tf_op jit(solution)/shard_map/all_gather | solution.py:67
  111.0 3.2 copy.61
  114.2 14.4 %all-to-all-start = ((bf16[128,32,256]{2,0,1:T(8,128)(2,1)}), bf16[128,32,256]{2,0,1:T(8,128)(2,1)}, u32[]{:S(2)}, u32[]{:S(2)}) async-start(bf16[128,32,256]{2,0,1:T(8,128)(2,1)} %bitcast.87), calls=%async_computation.2 | async-start | bytes 4194304 | tf_op jit(solution)/shard_map/all_to_all | solution.py:155
  128.5 0.0 reduce-scatter.3.cloned.1.call-start
  128.6 0.1 copy.28
  128.8 156.6 %all-gather.6.cloned.1.call-done = bf16[8192,64]{0,1:T(8,128)(2,1)} async-done(((bf16[256,64]{0,1:T(8,128)(2,1)}), bf16[8192,64]{0,1:T(8,128)(2,1)}) %all-gather.6.cloned.1.call-update) | async-done | bytes 1048592 | tf_op jit(solution)/shard_map/all_gather | solution.py:70
  285.4 2.1 convolution_convert_fusion.3
  287.5 21.9 %all_gather.17 = bf16[128,1024]{0,1:T(8,128)(2,1)S(1)} all-gather(bf16[128,64]{0,1:T(8,128)(2,1)S(1)} %convolution_convert_fusion.3), channel_id=1, replica_groups=mesh['dp'=32,'tensor'=16] {'tensor'}, dimensions={1}, use_global_device_ids=true | all-gather | bytes 278528 | tf_op jit(solution)/shard_map/all_gather | solution.py:78
  309.4 0.2 multiply_cosine_fusion
  309.6 0.1 copy.24
  309.7 0.1 copy.26
  309.8 122.8 %all-gather.8.cloned.1.call-done = bf16[8192,512]{1,0:T(8,128)(2,1)} async-done(((bf16[256,512]{1,0:T(8,128)(2,1)}), bf16[8192,512]{1,0:T(8,128)(2,1)}) %all-gather.8.cloned.1.call-update) | async-done | bytes 8388624 | tf_op jit(solution)/shard_map/all_gather | solution.py:69
  432.7 4.6 fusion.12
  437.3 0.1 reshape.74
  437.4 0.2 fusion.58
  437.6 0.1 subtract_convert_fusion.1
  437.7 0.3 fusion.27
  438.0 0.2 fusion.13
  438.2 0.2 fusion.8
  438.4 0.3 convolution_bitcast_fusion.3
  438.7 0.2 fusion.42
  439.0 0.2 fusion.14
  439.2 0.7 copy-done.3
  440.0 0.0 reduce-scatter.5.cloned.1.call-start
  440.0 0.2 convolution_bitcast_fusion
  440.3 0.1 add_convert_fusion
  440.4 0.1 pad_maximum_fusion.1
  440.5 0.1 copy.34
  440.7 8.3 %fusion.59 = f32[128,8192]{1,0:T(8,128)} fusion(bf16[128,512]{0,1:T(8,128)(2,1)S(1)} %bitcast.91, bf16[8192,512]{1,0:T(8,128)(2,1)} %all-gather.8.cloned.1.call-done), kind=kOutput, calls=%fused_computation.88 | convolution fusion | flops 1073741824 | bytes 12713984 | tf_op jit(solution)/shard_map/dot_general | solution.py:130
  449.0 72.2 %reduce-scatter.3.cloned.1.call-done = bf16[128,64]{0,1:T(8,128)(2,1)} async-done(((bf16[128,1024]{0,1:T(8,128)(2,1)}), bf16[128,64]{0,1:T(8,128)(2,1)}) %reduce-scatter.3.cloned.1.call-update) | async-done | bytes 16400 | tf_op jit(solution)/shard_map/reduce_scatter | solution.py:127
  521.1 4.3 fusion.1
  525.4 0.7 copy-done.5
  526.1 66.4 %all_gather.19 = bf16[4096,64]{0,1:T(8,128)(2,1)S(1)} all-gather(bf16[128,64]{0,1:T(8,128)(2,1)S(1)} %copy-done.5), channel_id=1, replica_groups=mesh['dp'=32,'tensor'=16] {'dp'}, dimensions={0}, use_global_device_ids=true | all-gather | bytes 540672 | tf_op jit(solution)/shard_map/all_gather | solution.py:154
  592.5 2.7 convolution_convert_fusion.2
  595.2 24.5 %reduce-scatter.5.cloned.1.call-done = bf16[512,128]{0,1:T(8,128)(2,1)} async-done(((bf16[8192,128]{0,1:T(8,128)(2,1)}), bf16[512,128]{0,1:T(8,128)(2,1)}) %reduce-scatter.5.cloned.1.call-update) | async-done | bytes 131088 | tf_op jit(solution)/shard_map/reduce_scatter | solution.py:134
  619.7 1.1 fusion.24
  620.8 33.6 %psum.22 = f32[128,1]{0,1:T(1,128)S(1)} all-reduce(f32[128,1]{0,1:T(1,128)S(1)} %bitcast.93), channel_id=1, replica_groups=mesh['dp'=32,'tensor'=16] {'tensor'}, use_global_device_ids=true, to_apply=%region_7.8 | all-reduce | flops 128 | bytes 1024 | tf_op jit(solution)/shard_map/psum | solution.py:149
  654.4 65.2 %psum.23 = f32[512]{0:T(512)} all-reduce(f32[512]{0:T(512)S(1)} %get-tuple-element.3), channel_id=1, replica_groups=mesh['dp'=32,'tensor'=16] {'dp'}, use_global_device_ids=true, to_apply=%region_9.10 | all-reduce | flops 512 | bytes 4096 | tf_op jit(solution)/shard_map/psum | solution.py:153
  719.6 1.7 fusion.23
  (22 shorter events, 0.2 us)
Async XLA Ops:
  7.2 103.8 %all-gather.4.cloned.1.call-start = ((), (), s32[]{:S(2)}) async-start(), calls=%async_computation.3 | async-start | bytes 2228224 | tf_op jit(solution)/shard_map/all_gather | solution.py:67
  45.8 239.6 %all-gather.6.cloned.1.call-start = ((), (), s32[]{:S(2)}) async-start(), calls=%async_computation.4 | async-start | bytes 1081344 | tf_op jit(solution)/shard_map/all_gather | solution.py:70
  46.6 386.1 %all-gather.8.cloned.1.call-start = ((), (), s32[]{:S(2)}) async-start(), calls=%async_computation.5 | async-start | bytes 8650752 | tf_op jit(solution)/shard_map/all_gather | solution.py:69
  114.2 14.4 %copy-start.4 = (bf16[128,512]{1,0:T(8,128)(2,1)S(1)}, bf16[128,512]{1,0:T(8,128)(2,1)}, u32[]{:S(2)}) copy-start(bf16[128,512]{1,0:T(8,128)(2,1)} %param.6) | copy-start | bytes 393220
  114.2 171.2 %copy-start = (bf16[128,8192]{1,0:T(8,128)(2,1)S(1)}, bf16[128,8192]{1,0:T(8,128)(2,1)}, u32[]{:S(2)}) copy-start(bf16[128,8192]{1,0:T(8,128)(2,1)} %all-gather.4.cloned.1.call-done) | copy-start | bytes 6291460
  114.2 478.4 %all-to-all-start = ((bf16[128,32,256]{2,0,1:T(8,128)(2,1)}), bf16[128,32,256]{2,0,1:T(8,128)(2,1)}, u32[]{:S(2)}, u32[]{:S(2)}) async-start(bf16[128,32,256]{2,0,1:T(8,128)(2,1)} %bitcast.87), calls=%async_computation.2 | async-start | bytes 4194304 | tf_op jit(solution)/shard_map/all_to_all | solution.py:155
  128.5 392.6 %reduce-scatter.3.cloned.1.call-start = ((), (), s32[]{:S(2)}) async-start(), calls=%async_computation.6 | async-start | bytes 278528 | tf_op jit(solution)/shard_map/reduce_scatter | solution.py:127
  439.2 0.7 copy-start.3
  440.0 179.7 %reduce-scatter.5.cloned.1.call-start = ((), (), s32[]{:S(2)}) async-start(), calls=%async_computation.7 | async-start | bytes 2228224 | tf_op jit(solution)/shard_map/reduce_scatter | solution.py:134
  440.7 80.5 %copy-start.1 = (bf16[8192,64]{0,1:T(8,128)(2,1)S(1)}, bf16[8192,64]{0,1:T(8,128)(2,1)}, u32[]{:S(2)}) copy-start(bf16[8192,64]{0,1:T(8,128)(2,1)} %all-gather.6.cloned.1.call-done) | copy-start | bytes 3145732
  525.4 0.7 copy-start.5
  526.1 93.5 %copy-start.2 = (bf16[128,512]{1,0:T(8,128)(2,1)S(1)}, bf16[128,512]{1,0:T(8,128)(2,1)}, u32[]{:S(2)}) copy-start(bf16[128,512]{1,0:T(8,128)(2,1)} %param.5) | copy-start | bytes 393220
Sparse Core Ops, SparseCore 0:
  45.9 65.0 all-gather.3
  113.0 172.3 all-gather.5
  287.5 145.1 all-gather.7
  440.1 80.9 reduce-scatter.2
  526.5 93.0 reduce-scatter.4
where the time goes:
time: 728 us
  waiting for transfers between devices  441 us (61%)
  blocking collectives  222 us (30%)
  matrix products  23.4 us (3%)
  starting transfers between devices  14.6 us (2%)
  between operations  14 us (2%)
    all_gather x1, waiting for transfers between devices, on_device(): lax.all_gather(w_keyval, 'dp', axis=0, tiled=True)  157 us
    all_gather x1, waiting for transfers between devices, on_device(): lax.all_gather(w_query, 'dp', axis=0, tiled=True)  123 us
    reduce_scatter x1, waiting for transfers between devices, on_device(): lax.psum_scatter(grad_terms.astype(jnp.bfloat16), 'tensor', scatter_dimen...  72.2 us
    all_gather x1, blocking collectives, on_device(): keyval_all = lax.all_gather(grad_keyval, 'dp', axis=0, tiled=True)  66.4 us
    psum x1, blocking collectives, on_device(): grad_gain = lax.psum(jnp.sum(grad_normed * unit_rows, axis=0), 'dp')  65.2 us
    all_gather x1, waiting for transfers between devices, on_device(): normed_full = lax.all_gather(normed, 'tensor', axis=1, tiled=True)  63.7 us
    psum x1, blocking collectives, on_device(): lax.psum(jnp.sum(as_float * as_float, axis=1, keepdims=True), 'tensor')  35.1 us
    psum x1, blocking collectives, on_device(): lax.psum(jnp.sum(scaled_grad * unit_rows, axis=1, keepdims=True), 'tensor')  33.6 us
  transfers between devices with their start and end apart: 6, of which 5 were waited for; matrix products, arithmetic and copies ran while one was open for 4% of the time, Pallas kernels for 0%

commit v1 on v0

--- a/solution.py
+++ b/solution.py
@@ -64,7 +64,9 @@
     inv_rms = lax.rsqrt(row_sum / model_width + 1e-05)
     unit_rows = as_float * inv_rms
     normed = (unit_rows * gain_local).astype(jnp.bfloat16)
-    normed_full = lax.all_gather(normed, "tensor", axis=1, tiled=True)
+    normed_full = jnp.concatenate(
+        lax.all_to_all(jnp.stack([normed] * lax.axis_size("tensor")), "tensor", 0, 0), axis=1
+    )
     query_weight, keyweight = (
         lax.all_gather(w_query, "dp", axis=0, tiled=True),
         lax.all_gather(w_keyval, "dp", axis=0, tiled=True),

time: 728 us -> 633 us (0.87)
  waiting for transfers between devices: 441 us -> 298 us
  blocking collectives: 222 us -> 270 us
    all_gather x1, waiting for transfers between devices: 157 us -> 74.4 us  [on_device(): lax.all_gather(w_keyval, 'dp', axis=0, tiled=True)]
    all_gather x1 -> x0, waiting for transfers between devices: 63.7 us -> none  [on_device(): normed_full = lax.all_gather(normed, 'tensor', axis=1, tiled=True)]
    all_to_all x0 -> x1, blocking collectives: none -> 33.8 us  [on_device(): lax.all_to_all(jnp.stack([normed] * lax.axis_size('tensor')), 'tensor', 0...]
    all_gather x1, blocking collectives: 21.9 us -> 35.5 us  [on_device(): keyval_full = lax.all_gather(keyval_part, 'tensor', axis=1, tiled=True)]
  transfers between devices with their start and end apart: 6 -> 5, of which waited for: 5 -> 4; matrix products, arithmetic and copies ran while one was open for 4% -> 5% of each run, Pallas kernels for 0% -> 0%
where the time goes in v1:
time: 633 us
  waiting for transfers between devices  298 us (47%)
  blocking collectives  270 us (43%)
  matrix products  24.4 us (4%)
  starting transfers between devices  15.4 us (2%)
  between operations  14 us (2%)
    all_gather x1, waiting for transfers between devices, on_device(): lax.all_gather(w_query, 'dp', axis=0, tiled=True)  128 us
    all_gather x1, waiting for transfers between devices, on_device(): lax.all_gather(w_keyval, 'dp', axis=0, tiled=True)  74.4 us
    reduce_scatter x1, waiting for transfers between devices, on_device(): lax.psum_scatter(grad_terms.astype(jnp.bfloat16), 'tensor', scatter_dimen...  71.6 us
    all_gather x1, blocking collectives, on_device(): keyval_all = lax.all_gather(grad_keyval, 'dp', axis=0, tiled=True)  66.4 us
    psum x1, blocking collectives, on_device(): grad_gain = lax.psum(jnp.sum(grad_normed * unit_rows, axis=0), 'dp')  65.2 us
    all_gather x1, blocking collectives, on_device(): keyval_full = lax.all_gather(keyval_part, 'tensor', axis=1, tiled=True)  35.5 us
    psum x1, blocking collectives, on_device(): lax.psum(jnp.sum(as_float * as_float, axis=1, keepdims=True), 'tensor')  35.1 us
    all_to_all x1, blocking collectives, on_device(): lax.all_to_all(jnp.stack([normed] * lax.axis_size('tensor')), 'tensor', 0...  33.8 us
  transfers between devices with their start and end apart: 5, of which 4 were waited for; matrix products, arithmetic and copies ran while one was open for 5% of the time, Pallas kernels for 0%

profile of v1, /device:TPU:16, one launch (start us, length us, event | category | flops | bytes accessed | tf_op | source)
XLA Modules:
  0.0 633.0 jit_solution(2102129585782429171)
XLA Ops:
  7.2 0.0 all-gather.3.cloned.1.call-start
  7.2 0.7 all-gather.3.cloned.1.call-update
  7.9 0.0 all-gather.5.cloned.1.call-start
  7.9 0.7 all-gather.5.cloned.1.call-update
  8.7 0.8 dynamic_slice.9
  9.4 1.0 fusion.25
  10.4 35.1 %psum.21 = f32[128,1]{0,1:T(1,128)S(1)} all-reduce(f32[128,1]{0,1:T(1,128)S(1)} %bitcast.94), channel_id=1, replica_groups=mesh['dp'=32,'tensor'=16] {'tensor'}, use_global_device_ids=true, to_apply=%region_1.0 | all-reduce | flops 128 | bytes 1024 | tf_op jit(solution)/shard_map/psum | solution.py:63
  45.6 1.0 fusion.19
  46.6 0.1 copy.23
  46.7 0.4 stack.2
  47.1 33.8 %all_to_all.24 = bf16[16,128,512]{1,2,0:T(8,128)(2,1)} all-to-all(bf16[16,128,512]{1,2,0:T(8,128)(2,1)S(1)} %stack.2), channel_id=1, replica_groups=mesh['dp'=32,'tensor'=16] {'tensor'}, dimensions={0} | all-to-all | bytes 4194304 | tf_op jit(solution)/shard_map/all_to_all | solution.py:68
  80.9 15.3 %all-to-all-start.1 = ((bf16[128,32,256]{0,2,1:T(8,128)(2,1)}), bf16[128,32,256]{0,2,1:T(8,128)(2,1)S(1)}, u32[]{:S(2)}, u32[]{:S(2)}) async-start(bf16[128,32,256]{0,2,1:T(8,128)(2,1)} %bitcast.22), calls=%async_computation.3 | async-start | bytes 4194304 | tf_op jit(solution)/shard_map/all_to_all | solution.py:157
  96.2 0.0 reduce-scatter.3.cloned.1.call-start
  96.2 0.1 copy.29
  96.4 74.4 %all-gather.3.cloned.1.call-done = bf16[8192,64]{0,1:T(8,128)(2,1)} async-done(((bf16[256,64]{0,1:T(8,128)(2,1)}), bf16[8192,64]{0,1:T(8,128)(2,1)}) %all-gather.3.cloned.1.call-update) | async-done | bytes 1048592 | tf_op jit(solution)/shard_map/all_gather | solution.py:72
  170.9 2.4 convolution_convert_fusion.3
  173.3 35.5 %all_gather.13 = bf16[128,1024]{0,1:T(8,128)(2,1)S(1)} all-gather(bf16[128,64]{0,1:T(8,128)(2,1)S(1)} %convolution_convert_fusion.3), channel_id=1, replica_groups=mesh['dp'=32,'tensor'=16] {'tensor'}, dimensions={1}, use_global_device_ids=true | all-gather | bytes 278528 | tf_op jit(solution)/shard_map/all_gather | solution.py:80
  208.8 0.2 multiply_cosine_fusion
  209.0 0.1 copy.25
  209.1 0.1 copy.27
  209.2 128.4 %all-gather.5.cloned.1.call-done = bf16[8192,512]{1,0:T(8,128)(2,1)} async-done(((bf16[256,512]{1,0:T(8,128)(2,1)}), bf16[8192,512]{1,0:T(8,128)(2,1)}) %all-gather.5.cloned.1.call-update) | async-done | bytes 8388624 | tf_op jit(solution)/shard_map/all_gather | solution.py:71
  337.6 5.3 fusion.12
  342.9 0.1 reshape.85
  343.0 0.2 fusion.58
  343.2 0.1 subtract_convert_fusion.1
  343.3 0.3 fusion.27
  343.6 0.2 fusion.13
  343.8 0.2 fusion.8
  344.1 0.3 convolution_bitcast_fusion.3
  344.4 0.2 fusion.42
  344.7 0.2 fusion.14
  344.9 0.7 copy-done.2
  345.6 0.0 reduce-scatter.5.cloned.1.call-start
  345.6 0.2 convolution_bitcast_fusion
  345.9 0.1 add_convert_fusion
  346.0 0.1 pad_maximum_fusion.1
  346.2 0.1 copy.35
  346.3 8.3 %fusion.59 = f32[128,8192]{1,0:T(8,128)} fusion(bf16[128,512]{0,1:T(8,128)(2,1)S(1)} %bitcast.91, bf16[8192,512]{1,0:T(8,128)(2,1)} %all-gather.5.cloned.1.call-done), kind=kOutput, calls=%fused_computation.87 | convolution fusion | flops 1073741824 | bytes 12713984 | tf_op jit(solution)/shard_map/dot_general | solution.py:132
  354.6 71.6 %reduce-scatter.3.cloned.1.call-done = bf16[128,64]{0,1:T(8,128)(2,1)} async-done(((bf16[128,1024]{0,1:T(8,128)(2,1)}), bf16[128,64]{0,1:T(8,128)(2,1)}) %reduce-scatter.3.cloned.1.call-update) | async-done | bytes 16400 | tf_op jit(solution)/shard_map/reduce_scatter | solution.py:129
  426.2 4.3 fusion.1
  430.5 2.9 copy.40
  433.5 66.4 %all_gather.15 = bf16[4096,64]{0,1:T(8,128)(2,1)S(1)} all-gather(bf16[128,64]{0,1:T(8,128)(2,1)S(1)} %copy-done.4), channel_id=1, replica_groups=mesh['dp'=32,'tensor'=16] {'dp'}, dimensions={0}, use_global_device_ids=true | all-gather | bytes 540672 | tf_op jit(solution)/shard_map/all_gather | solution.py:156
  499.8 2.7 convolution_convert_fusion.2
  502.5 22.3 %reduce-scatter.5.cloned.1.call-done = bf16[512,128]{0,1:T(8,128)(2,1)} async-done(((bf16[8192,128]{0,1:T(8,128)(2,1)}), bf16[512,128]{0,1:T(8,128)(2,1)}) %reduce-scatter.5.cloned.1.call-update) | async-done | bytes 131088 | tf_op jit(solution)/shard_map/reduce_scatter | solution.py:136
  524.8 1.1 fusion.24
  525.9 33.6 %psum.22 = f32[128,1]{0,1:T(1,128)S(1)} all-reduce(f32[128,1]{0,1:T(1,128)S(1)} %bitcast.93), channel_id=1, replica_groups=mesh['dp'=32,'tensor'=16] {'tensor'}, use_global_device_ids=true, to_apply=%region_7.8 | all-reduce | flops 128 | bytes 1024 | tf_op jit(solution)/shard_map/psum | solution.py:151
  559.6 65.2 %psum.23 = f32[512]{0:T(512)} all-reduce(f32[512]{0:T(512)S(1)} %get-tuple-element.3), channel_id=1, replica_groups=mesh['dp'=32,'tensor'=16] {'dp'}, use_global_device_ids=true, to_apply=%region_9.10 | all-reduce | flops 512 | bytes 4096 | tf_op jit(solution)/shard_map/psum | solution.py:155
  624.8 1.7 fusion.23
  (20 shorter events, 0.2 us)
Async XLA Ops:
  7.2 163.7 %all-gather.3.cloned.1.call-start = ((), (), s32[]{:S(2)}) async-start(), calls=%async_computation.4 | async-start | bytes 1081344 | tf_op jit(solution)/shard_map/all_gather | solution.py:72
  7.9 329.7 %all-gather.5.cloned.1.call-start = ((), (), s32[]{:S(2)}) async-start(), calls=%async_computation.5 | async-start | bytes 8650752 | tf_op jit(solution)/shard_map/all_gather | solution.py:71
  80.9 15.4 %copy-start.3 = (bf16[128,512]{1,0:T(8,128)(2,1)S(1)}, bf16[128,512]{1,0:T(8,128)(2,1)}, u32[]{:S(2)}) copy-start(bf16[128,512]{1,0:T(8,128)(2,1)} %param.6) | copy-start | bytes 393220
  80.9 349.6 %all-to-all-start.1 = ((bf16[128,32,256]{0,2,1:T(8,128)(2,1)}), bf16[128,32,256]{0,2,1:T(8,128)(2,1)S(1)}, u32[]{:S(2)}, u32[]{:S(2)}) async-start(bf16[128,32,256]{0,2,1:T(8,128)(2,1)} %bitcast.22), calls=%async_computation.3 | async-start | bytes 4194304 | tf_op jit(solution)/shard_map/all_to_all | solution.py:157
  96.2 330.0 %reduce-scatter.3.cloned.1.call-start = ((), (), s32[]{:S(2)}) async-start(), calls=%async_computation.6 | async-start | bytes 278528 | tf_op jit(solution)/shard_map/reduce_scatter | solution.py:129
  344.9 0.7 copy-start.2
  345.6 179.2 %reduce-scatter.5.cloned.1.call-start = ((), (), s32[]{:S(2)}) async-start(), calls=%async_computation.7 | async-start | bytes 2228224 | tf_op jit(solution)/shard_map/reduce_scatter | solution.py:136
  346.3 79.9 %copy-start = (bf16[8192,64]{0,1:T(8,128)(2,1)S(1)}, bf16[8192,64]{0,1:T(8,128)(2,1)}, u32[]{:S(2)}) copy-start(bf16[8192,64]{0,1:T(8,128)(2,1)} %all-gather.3.cloned.1.call-done) | copy-start | bytes 3145732
  430.5 2.9 copy-start.4
  433.5 91.4 %copy-start.1 = (bf16[128,512]{1,0:T(8,128)(2,1)S(1)}, bf16[128,512]{1,0:T(8,128)(2,1)}, u32[]{:S(2)}) copy-start(bf16[128,512]{1,0:T(8,128)(2,1)} %param.5) | copy-start | bytes 393220
Sparse Core Ops, SparseCore 0:
  10.0 160.8 all-gather.2
  172.9 164.6 all-gather.4
  345.7 80.4 reduce-scatter.2
  431.6 93.1 reduce-scatter.4
